TPU v7x, 32 devices: a whole 2x2x4 slice. The times are simulated.
32 devices in a mesh: layer: 2 (over x), row: 16 (over z, y, core).
Axes of the slice: x: 2, y: 2, z: 4, core: 2. Of those that a mesh axis runs over, the one named last changes fastest.
Arguments:
- leaf_rhs: float32 [2, 16, 256, 384], P('layer', 'row'), may hold values from -6 to 6
- leaf_inverse: float32 [2, 16, 256, 256], P('layer', 'row'), may hold values from -0.375 to 0.375
- leaf_coupling: float32 [2, 16, 4, 512, 256], P('layer', 'row'), may hold values from -0.09375 to 0.09375
- parent: int32 [2, 16], P('layer', 'row'), may hold values from 0 to 3
- sep_rhs: float32 [2, 4, 512, 384], P('layer', None, 'row'), may hold values from -6 to 6
- sep_inverse: float32 [2, 4, 512, 512], P('layer', None, 'row'), may hold values from -0.25 to 0.25
- sep_coupling: float32 [2, 3, 512, 512], P('layer', None, 'row'), may hold values from -0.125 to 0.125
- root_coupling: float32 [2, 512, 512], P('layer', 'row'), may hold values from -0.1875 to 0.1875
- root_rhs: float32 [512, 384], P('row'), may hold values from -6 to 6
- root_inverse: float32 [512, 512], P('row'), may hold values from -0.25 to 0.25
Outputs:
- sep_solution: float32 [2, 4, 512, 384], P('layer', None, 'row')
- root_solution: float32 [512, 384], P('row')
All inputs are finite; a program needn't handle non-finite values.
Results may differ from a plain program's by a relative error of at most 0.0003.
Values sent between devices are 32-bit elements; how exact they have to be, the bound alone decides.
A program may use at most 64 MiB of HBM per device.

v0:
```python
import jax
import jax.numpy as jnp
from jax import lax
from jax.sharding import PartitionSpec as P


def body(
    leaf_rhs,
    leaf_inverse,
    leaf_coupling,
    parent,
    sep_rhs,
    sep_inverse,
    sep_coupling,
    root_coupling,
    root_rhs,
    root_inverse,
):
    highest = lax.Precision.HIGHEST
    sep_count = sep_rhs.shape[1]
    row_count = sep_rhs.shape[2]
    row_start = lax.axis_index("row") * row_count
    leaf_solution = jnp.dot(leaf_inverse[0, 0], leaf_rhs[0, 0], precision=highest)
    levels = jnp.arange(sep_count, dtype=jnp.int32)
    keep_mask = (levels >= parent[0, 0]).astype(jnp.float32)

    def residual_term(k):
        coupled = jnp.dot(leaf_coupling[0, 0, k], leaf_solution, precision=highest) * keep_mask[k]
        own_rhs = lax.dynamic_update_slice_in_dim(
            jnp.zeros_like(coupled), sep_rhs[0, k], row_start, 0
        )
        return own_rhs - coupled

    residual_list = [lax.psum(residual_term(k), "row") for k in range(sep_count)]
    local_rows = [
        jnp.dot(sep_inverse[0, k], residual_list[k], precision=highest) for k in range(sep_count)
    ]
    solved = []
    gathered = None
    for k in range(sep_count):
        current = local_rows[k]
        if k > 0:
            current = current - jnp.dot(sep_coupling[0, k - 1], gathered, precision=highest)
        solved.append(current)
        gathered = lax.all_gather(current, "row", axis=0, tiled=True)
    sep_out = jnp.stack(solved)[None]
    root_term = jnp.dot(root_coupling[0], gathered, precision=highest)
    root_sum = lax.psum(root_term, "layer")
    root_residual = root_rhs - root_sum
    root_out = jnp.dot(
        root_inverse, lax.all_gather(root_residual, "row", axis=0, tiled=True), precision=highest
    )
    return (sep_out, root_out)


def solution(mesh):
    return jax.shard_map(
        body,
        mesh=mesh,
        in_specs=(
            P("layer", "row", None, None),
            P("layer", "row", None, None),
            P("layer", "row", None, None, None),
            P("layer", "row"),
            P("layer", None, "row", None),
            P("layer", None, "row", None),
            P("layer", None, "row", None),
            P("layer", "row", None),
            P("row", None),
            P("row", None),
        ),
        out_specs=(P("layer", None, "row", None), P("row", None)),
        check_vma=False,
    )
```

profile of v0, /device:TPU:0, one launch (start us, length us, event | category | flops | bytes accessed | tf_op | source)
XLA Modules:
  0.0 256.8 jit_solution(18028088945039501425)
XLA Ops:
  7.2 0.0 copy-start
  7.2 0.0 copy-start.6
  7.2 0.0 copy-start.5
  7.2 0.0 all-reduce.3.cloned.1.call-start
  8.0 0.7 fusion.38
  8.6 0.1 broadcast.11.clone.2
  8.7 0.0 copy-start.1
  8.7 1.0 bitcast_dynamic-update-slice_fusion.2
  9.7 0.1 broadcast.11.clone.1
  9.7 0.8 bitcast_dynamic-update-slice_fusion.1
  10.5 0.1 broadcast.11.clone
  10.6 0.0 copy-done.6
  10.6 0.1 broadcast.11.clone.3
  10.7 0.0 copy-done
  10.7 0.0 copy-done.5
  10.7 0.6 fusion.16
  11.3 0.0 copy-done.1
  11.3 2.6 %fusion.5 = f32[512,384]{1,0:T(8,128)} fusion(f32[512,384]{1,0:T(8,128)S(1)} %bitcast_dynamic-update-slice_fusion.2, f32[256,384]{1,0:T(8,128)S(1)} %fusion.16, f32[1,1,4,512,256]{4,3,2,1,0:T(8,128)S(1)} %copy-done.1, f32[]{:T(128)} %bitcast.12), kind=kOutput, calls=%fused_computation.9 | convolution fusion | flops 604372992 | bytes 2490372 | tf_op jit(solution)/shard_map/dot_general | solution.py:28
  13.9 2.6 %fusion.6 = f32[512,384]{1,0:T(8,128)} fusion(f32[512,384]{1,0:T(8,128)S(1)} %bitcast_dynamic-update-slice_fusion.1, f32[256,384]{1,0:T(8,128)S(1)} %fusion.16, f32[1,1,4,512,256]{4,3,2,1,0:T(8,128)S(1)} %copy-done.1, f32[]{:T(128)} %bitcast.20), kind=kOutput, calls=%fused_computation.10 | convolution fusion | flops 604372992 | bytes 2490372 | tf_op jit(solution)/shard_map/dot_general | solution.py:28
  16.5 2.6 %fusion.7 = f32[512,384]{1,0:T(8,128)} fusion(f32[512,384]{1,0:T(8,128)S(1)} %bitcast_dynamic-update-slice_fusion, f32[256,384]{1,0:T(8,128)S(1)} %fusion.16, f32[1,1,4,512,256]{4,3,2,1,0:T(8,128)S(1)} %copy-done.1, f32[]{:T(128)} %bitcast.28), kind=kOutput, calls=%fused_computation.11 | convolution fusion | flops 604372992 | bytes 2490372 | tf_op jit(solution)/shard_map/dot_general | solution.py:28
  19.1 2.6 fusion.4
  21.6 0.0 copy-start.4
  21.6 0.0 all-reduce.3.cloned.1.call-update
  21.7 107.3 %all-reduce.3.cloned.1.call-done = (f32[512,384]{1,0:T(8,128)}, f32[512,384]{1,0:T(8,128)}, f32[512,384]{1,0:T(8,128)}, f32[512,384]{1,0:T(8,128)}) async-done(((f32[512,384]{1,0:T(8,128)}, f32[512,384]{1,0:T(8,128)}, f32[512,384]{1,0:T(8,128)}, f32[512,384]{1,0:T(8,128)}), (f32[512,384]{1,0:T(8,128)}, f32[512,384]{1,0:T(8,128)}, f32[512,384]{1,0:T(8,128)}, ...) | async-done | bytes 3145744 | tf_op jit(solution)/shard_map/psum | solution.py:34
  129.0 0.0 copy-start.3
  129.0 0.0 copy-start.2
  129.0 0.0 copy-done.4
  129.0 0.0 copy-start.7
  129.0 1.8 fusion.21
  130.8 1.7 fusion.29
  132.5 0.0 copy-done.3
  132.5 0.5 fusion.24
  133.0 0.0 copy-done.2
  133.1 0.5 fusion.27
  133.6 21.6 %all_gather.15 = f32[512,384]{1,0:T(8,128)S(1)} all-gather(f32[32,384]{1,0:T(8,128)S(1)} %bitcast.104), channel_id=1, replica_groups=mesh['layer'=2,'row'=16] {'row'}, dimensions={0}, use_global_device_ids=true | all-gather | bytes 835584 | tf_op jit(solution)/shard_map/all_gather | solution.py:45
  155.2 0.0 copy-done.7
  155.2 0.5 convolution_subtract_fusion.2
  155.8 0.0 copy-start.8
  155.8 19.6 %all_gather.16 = f32[512,384]{1,0:T(8,128)S(1)} all-gather(f32[32,384]{1,0:T(8,128)S(1)} %bitcast.106), channel_id=1, replica_groups=mesh['layer'=2,'row'=16] {'row'}, dimensions={0}, use_global_device_ids=true | all-gather | bytes 835584 | tf_op jit(solution)/shard_map/all_gather | solution.py:45
  175.4 0.0 copy-start.10
  175.4 0.5 convolution_subtract_fusion.1
  175.9 0.0 copy-start.9
  175.9 21.8 %all_gather.17 = f32[512,384]{1,0:T(8,128)S(1)} all-gather(f32[32,384]{1,0:T(8,128)S(1)} %bitcast.108), channel_id=1, replica_groups=mesh['layer'=2,'row'=16] {'row'}, dimensions={0}, use_global_device_ids=true | all-gather | bytes 835584 | tf_op jit(solution)/shard_map/all_gather | solution.py:45
  197.7 0.5 convolution_subtract_fusion
  198.3 19.6 %all_gather.18 = f32[512,384]{1,0:T(8,128)S(1)} all-gather(f32[32,384]{1,0:T(8,128)S(1)} %bitcast.110), channel_id=1, replica_groups=mesh['layer'=2,'row'=16] {'row'}, dimensions={0}, use_global_device_ids=true | all-gather | bytes 835584 | tf_op jit(solution)/shard_map/all_gather | solution.py:45
  217.9 0.0 copy-done.8
  217.9 0.5 convolution_bitcast_fusion.1
  218.4 8.6 %psum.39 = f32[32,384]{1,0:T(8,128)S(1)} all-reduce(f32[32,384]{1,0:T(8,128)S(1)} %convolution_bitcast_fusion.1), channel_id=1, replica_groups=mesh['layer'=2,'row'=16] {'layer'}, use_global_device_ids=true, to_apply=%region_4.0 | all-reduce | flops 12288 | bytes 98304 | tf_op jit(solution)/shard_map/psum | solution.py:48
  227.0 0.0 copy-done.10
  227.0 21.1 %all_gather.19 = f32[512,384]{1,0:T(8,128)S(1)} all-gather(f32[32,384]{1,0:T(8,128)S(1)} %sub.43), channel_id=1, replica_groups=mesh['layer'=2,'row'=16] {'row'}, dimensions={0}, use_global_device_ids=true | all-gather | bytes 835584 | tf_op jit(solution)/shard_map/all_gather | solution.py:51
  248.1 0.0 copy-done.9
  248.1 1.2 convolution_bitcast_fusion
  249.3 0.7 maximum_bitcast_fusion
  (4 shorter events, 0.0 us)
Async XLA Ops:
  7.2 3.5 %copy-start = (f32[1,1,256,384]{3,2,1,0:T(8,128)S(1)}, f32[1,1,256,384]{3,2,1,0:T(8,128)}, u32[]{:S(2)}) copy-start(f32[1,1,256,384]{3,2,1,0:T(8,128)} %param.10) | copy-start | bytes 1179652
  7.2 3.4 %copy-start.6 = (f32[1,4,32,384]{3,2,1,0:T(8,128)S(1)}, f32[1,4,32,384]{3,2,1,0:T(8,128)}, u32[]{:S(2)}) copy-start(f32[1,4,32,384]{3,2,1,0:T(8,128)} %param.14) | copy-start | bytes 589828
  7.2 3.5 %copy-start.5 = (f32[1,1,256,256]{3,2,1,0:T(8,128)S(1)}, f32[1,1,256,256]{3,2,1,0:T(8,128)}, u32[]{:S(2)}) copy-start(f32[1,1,256,256]{3,2,1,0:T(8,128)} %param.11) | copy-start | bytes 786436
  7.2 121.8 %all-reduce.3.cloned.1.call-start = ((), (), s32[]{:S(2)}) async-start(), calls=%async_computation | async-start | bytes 6291456 | tf_op jit(solution)/shard_map/psum | solution.py:34
  8.7 2.6 %copy-start.1 = (f32[1,1,4,512,256]{4,3,2,1,0:T(8,128)S(1)}, f32[1,1,4,512,256]{4,3,2,1,0:T(8,128)}, u32[]{:S(2)}) copy-start(f32[1,1,4,512,256]{4,3,2,1,0:T(8,128)} %param.12) | copy-start | bytes 6291460
  21.6 107.4 %copy-start.4 = (f32[1,4,32,512]{3,2,1,0:T(8,128)S(1)}, f32[1,4,32,512]{3,2,1,0:T(8,128)}, u32[]{:S(2)}) copy-start(f32[1,4,32,512]{3,2,1,0:T(8,128)} %param.15) | copy-start | bytes 786436
  129.0 3.5 %copy-start.3 = (f32[512,384]{1,0:T(8,128)S(1)}, f32[512,384]{1,0:T(8,128)}, u32[]{:S(2)}) copy-start(f32[512,384]{1,0:T(8,128)} %get-tuple-element.3) | copy-start | bytes 2359300
  129.0 4.1 %copy-start.2 = (f32[512,384]{1,0:T(8,128)S(1)}, f32[512,384]{1,0:T(8,128)}, u32[]{:S(2)}) copy-start(f32[512,384]{1,0:T(8,128)} %get-tuple-element.4) | copy-start | bytes 2359300
  129.0 26.2 %copy-start.7 = (f32[1,3,32,512]{3,2,1,0:T(8,128)S(1)}, f32[1,3,32,512]{3,2,1,0:T(8,128)}, u32[]{:S(2)}) copy-start(f32[1,3,32,512]{3,2,1,0:T(8,128)} %param.16) | copy-start | bytes 589828
  155.8 62.1 %copy-start.8 = (f32[1,32,512]{2,1,0:T(8,128)S(1)}, f32[1,32,512]{2,1,0:T(8,128)}, u32[]{:S(2)}) copy-start(f32[1,32,512]{2,1,0:T(8,128)} %param.17) | copy-start | bytes 196612
  175.4 51.6 %copy-start.10 = (f32[32,384]{1,0:T(8,128)S(1)}, f32[32,384]{1,0:T(8,128)}, u32[]{:S(2)}) copy-start(f32[32,384]{1,0:T(8,128)} %param.18) | copy-start | bytes 147460
  175.9 72.2 %copy-start.9 = (f32[32,512]{1,0:T(8,128)S(1)}, f32[32,512]{1,0:T(8,128)}, u32[]{:S(2)}) copy-start(f32[32,512]{1,0:T(8,128)} %param.19) | copy-start | bytes 196612
Sparse Core Ops, SparseCore 0:
  21.8 107.1 all-reduce.2
where the time goes:
time: 257 us
  blocking collectives  112 us (44%)
  waiting for transfers between devices  107 us (42%)
  matrix products  18.8 us (7%)
  between operations  15 us (6%)
  local copies, waits for them, and re-layouts  2.71 us (1%)
    psum x1, waiting for transfers between devices, body(): lax.psum(residual_term(k), 'row')  107 us
    all_gather x4, blocking collectives, body(): gathered = lax.all_gather(current, 'row', axis=0, tiled=True)  82.6 us
    all_gather x1, blocking collectives, body(): lax.all_gather(root_residual, 'row', axis=0, tiled=True)  21.1 us
    dot_general x4, matrix products, residual_term(): jnp.dot(leaf_coupling[0, 0, k], leaf_solution, precision=highest)  10.3 us
    psum x1, blocking collectives, body(): root_sum = lax.psum(root_term, 'layer')  8.58 us
  transfers between devices with their start and end apart: 1, of which 1 were waited for; matrix products, arithmetic and copies ran while one was open for 0% of the time, Pallas kernels for 0%

commit v1 on v0

--- a/solution.py
+++ b/solution.py
@@ -1,7 +1,448 @@
+import functools
+
 import jax
 import jax.numpy as jnp
 from jax import lax
+from jax.experimental import pallas as pl
+from jax.experimental.pallas import tpu as pltpu
 from jax.sharding import PartitionSpec as P
+
+MESH = pl.DeviceIdType.MESH
+NN = (((1,), (0,)), ((), ()))
+NT = (((1,), (1,)), ((), ()))
+HALVES = 2
+LAG = 1
+
+
+def split(a):
+    high = a.astype(jnp.bfloat16)
+    return high, (a - high.astype(jnp.float32)).astype(jnp.bfloat16)
+
+
+def dot3(a, b, dims):
+    (ah, al), (bh, bl) = a, b
+    dot = functools.partial(lax.dot_general, dimension_numbers=dims, preferred_element_type=jnp.float32)
+    return dot(ah, bh) + (dot(ah, bl) + dot(al, bh))
+
+
+def kernel(
+    n_z,
+    parent,
+    leaf_rhs,
+    leaf_inverse,
+    leaf_coupling,
+    sep_rhs,
+    sep_inverse,
+    sep_coupling,
+    root_coupling,
+    root_rhs,
+    root_inverse,
+    sep_out,
+    root_out,
+    g_inv,
+    g_chain,
+    g_rc,
+    g_rr,
+    g_ri,
+    part,
+    from_core,
+    to_y,
+    from_y,
+    mine,
+    fwd,
+    bwd,
+    from_left,
+    from_right,
+    total,
+    solved,
+    padded,
+    turned,
+    pieces,
+    root_send,
+    root_recv,
+    root_full,
+    w_send,
+    w_recv,
+    c_send,
+    c_recv,
+    y_send,
+    y_recv,
+    f_send,
+    f_recv,
+    b_send,
+    b_recv,
+    a_send,
+    a_recv,
+    o_send,
+    o_recv,
+    x_send,
+    x_recv,
+):
+    seps, rows, right = sep_rhs.shape
+    width = sep_inverse.shape[2]
+    zrows = width // n_z
+    half, quarter = right // 2, right // 4
+    sub = quarter // HALVES
+
+    layer = lax.axis_index("layer")
+    me = lax.axis_index("row")
+    z, y, c = me // 4, (me // 2) % 2, me % 2
+    plane = 2 * y + c
+    base = 4 * z
+
+    def at(zz, yy, cc):
+        return (layer, 4 * zz + 2 * yy + cc)
+
+    core_peer = at(z, y, 1 - c)
+    y_peer = at(z, 1 - y, c)
+    far_peer = at(z, 1 - y, 1 - c)
+    x_peer = (1 - layer, me)
+    left, right_peer = (layer, me - 4), (layer, me + 4)
+    z_peers = [at((z + d) % n_z, y, c) for d in range(1, n_z)]
+    plane_peers = [core_peer, y_peer, far_peer]
+
+    def remote(src, dst, send, recv, peer):
+        return pltpu.make_async_remote_copy(
+            src_ref=src, dst_ref=dst, send_sem=send, recv_sem=recv, device_id=peer, device_id_type=MESH
+        )
+
+    barrier = pltpu.get_barrier_semaphore()
+    peers = plane_peers + z_peers + [x_peer]
+    for peer in peers:
+        pl.semaphore_signal(barrier, inc=1, device_id=peer, device_id_type=MESH)
+    pl.semaphore_wait(barrier, len(peers))
+
+    own_rows = pl.ds(pl.multiple_of(plane * rows, rows), rows)
+    y_rows = pl.ds(pl.multiple_of((2 * (1 - y) + c) * rows, rows), rows)
+    weights = [
+        (sep_inverse, g_inv, True),
+        (sep_coupling, g_chain, True),
+        (root_coupling, g_rc, False),
+        (root_rhs, g_rr, False),
+        (root_inverse, g_ri, False),
+    ]
+
+    def slot(ref, deep, where):
+        return ref.at[:, where, :] if deep else ref.at[where, :]
+
+    def weight(way, n):
+        source, dest, deep = weights[n]
+        if way == 2:
+            source, where = slot(dest, deep, y_rows), y_rows
+        else:
+            where = own_rows
+        return remote(
+            source,
+            slot(dest, deep, where),
+            w_send.at[way, n],
+            w_recv.at[way, n],
+            y_peer if way == 0 else core_peer,
+        )
+
+    def weight_start(way, which):
+        for n in which:
+            weight(way, n).start()
+
+    weight_start(0, (0,))
+    g_inv[:, own_rows, :] = sep_inverse[...]
+    g_chain[:, own_rows, :] = sep_coupling[...]
+    g_rc[own_rows, :] = root_coupling[...]
+    g_rr[own_rows, :] = root_rhs[...]
+    g_ri[own_rows, :] = root_inverse[...]
+
+    leaf = dot3(split(leaf_inverse[...]), split(leaf_rhs[...]), NN)
+    leaf_t = split(leaf.T)
+    zlanes = pl.ds(pl.multiple_of(z * zrows, 128), zrows)
+    core_cols = pl.ds(pl.multiple_of(half * c, 8), half)
+    other_core_cols = pl.ds(pl.multiple_of(half * (1 - c), 8), half)
+    padded[...] = jnp.zeros_like(padded)
+
+    def core_copy(k):
+        return remote(
+            part.at[k, other_core_cols, :], from_core.at[k], c_send.at[k], c_recv.at[k], core_peer
+        )
+
+    def stage_a(k):
+        keep = jnp.where(parent[0, 0] <= k, -1.0, 0.0).astype(jnp.float32)
+        part[k] = dot3(leaf_t, split(leaf_coupling[k]), NT) * keep
+        padded[own_rows, :] = sep_rhs[k]
+        part[k, :, zlanes] += padded[...].T
+        core_copy(k).start()
+
+    own_y = pl.multiple_of(quarter * y, 8)
+    peer_y = pl.multiple_of(quarter * (1 - y), 8)
+
+    def y_copy(k, h):
+        where = pl.ds(h * sub, sub)
+        return remote(
+            to_y.at[k, where, :], from_y.at[k, where, :], y_send.at[k, h], y_recv.at[k, h], y_peer
+        )
+
+    def stage_b(k):
+        core_copy(k).wait_recv()
+        to_y[k] = (
+            part[k, pl.ds(pl.multiple_of(half * c + peer_y, 8), quarter), :]
+            + from_core[k, pl.ds(peer_y, quarter), :]
+        )
+        for h in range(HALVES):
+            y_copy(k, h).start()
+
+    def fwd_copy(k, h):
+        where = pl.ds(h * sub, sub)
+        return remote(
+            fwd.at[k, where, :], from_left.at[k, where, :], f_send.at[k, h], f_recv.at[k, h], right_peer
+        )
+
+    def bwd_copy(k, h):
+        where = pl.ds(h * sub, sub)
+        return remote(
+            bwd.at[k, where, :], from_right.at[k, where, :], b_send.at[k, h], b_recv.at[k, h], left
+        )
+
+    def stage_c(k, h):
+        where = pl.ds(h * sub, sub)
+        y_copy(k, h).wait_recv()
+        mine[k, where, :] = (
+            part[k, pl.ds(pl.multiple_of(half * c + own_y + h * sub, 8), sub), :]
+            + from_core[k, pl.ds(pl.multiple_of(own_y + h * sub, 8), sub), :]
+            + from_y[k, where, :]
+        )
+
+    def hop(k, h, number):
+        where = pl.ds(h * sub, sub)
+
+        @pl.when(z == number)
+        def _():
+            if number == 0:
+                fwd[k, where, :] = mine[k, where, :]
+            else:
+                fwd_copy(k, h).wait_recv()
+                fwd[k, where, :] = mine[k, where, :] + from_left[k, where, :]
+            fwd_copy(k, h).start()
+
+        @pl.when(z == n_z - 1 - number)
+        def _():
+            if number == 0:
+                bwd[k, where, :] = mine[k, where, :]
+            else:
+                bwd_copy(k, h).wait_recv()
+                bwd[k, where, :] = mine[k, where, :] + from_right[k, where, :]
+            bwd_copy(k, h).start()
+
+    def finish(k, h):
+        where = pl.ds(h * sub, sub)
+
+        @pl.when(z == 0)
+        def _():
+            bwd_copy(k, h).wait_recv()
+            total[k, where, :] = mine[k, where, :] + from_right[k, where, :]
+
+        @pl.when(z == n_z - 1)
+        def _():
+            fwd_copy(k, h).wait_recv()
+            total[k, where, :] = mine[k, where, :] + from_left[k, where, :]
+
+        @pl.when(jnp.logical_and(z > 0, z < n_z - 1))
+        def _():
+            total[k, where, :] = mine[k, where, :] + (from_left[k, where, :] + from_right[k, where, :])
+
+    def z_lanes(zz):
+        return pl.ds(pl.multiple_of(zz * zrows, 128), zrows)
+
+    def along_z(ref, k, d, sender):
+        where = z_lanes((z - d + n_z) % n_z if sender else z)
+        return remote(
+            ref.at[:, where], ref.at[:, where], a_send.at[k, d - 1], a_recv.at[k, d - 1], z_peers[d - 1]
+        )
+
+    def out_copy(k, n):
+        peer_plane = (2 * y + 1 - c, 2 * (1 - y) + c, 2 * (1 - y) + 1 - c)[n]
+        rows_there = pl.ds(pl.multiple_of(peer_plane * rows, rows), rows)
+        return remote(
+            turned.at[k, rows_there, :], pieces.at[k, n], o_send.at[k, n], o_recv.at[k, n], plane_peers[n]
+        )
+
+    def turn(k, value):
+        turned[k, :, pl.ds(0, quarter)] = value.T
+        for n in range(3):
+            out_copy(k, n).start()
+
+    def assemble(k):
+        for n in range(3):
+            out_copy(k, n).wait_recv()
+        own = turned[k, own_rows, :][:, :quarter]
+        by_core, by_y, by_far = (pieces[k, n][:, :quarter] for n in range(3))
+        low_y, low_core = y == 0, c == 0
+        same = (jnp.where(low_y, own, by_y), jnp.where(low_y, by_y, own))
+        other = (jnp.where(low_y, by_core, by_far), jnp.where(low_y, by_far, by_core))
+        blocks = [jnp.where(low_core, same[n], other[n]) for n in range(2)]
+        blocks += [jnp.where(low_core, other[n], same[n]) for n in range(2)]
+        return jnp.concatenate(blocks, axis=1)
+
+    def wait_along_z(ref, k):
+        for d in range(1, n_z):
+            along_z(ref, k, d, True).wait_recv()
+
+    def chain(k):
+        value = dot3(split(total[k]), split(g_inv[k]), NT)
+        if k > 0:
+            wait_along_z(solved.at[k - 1], k - 1)
+            value = value - dot3(split(solved[k - 1]), split(g_chain[k - 1]), NT)
+        solved[k, :, zlanes] = value
+        for d in range(1, n_z):
+            along_z(solved.at[k], k, d, False).start()
+        turn(k, value)
+
+    stage_a(0)
+    weight_start(1, (0,))
+    stage_a(1)
+    stage_b(0)
+    stage_a(2)
+    stage_b(1)
+    stage_a(3) if seps > 3 else None
+    weight_start(0, (1, 2, 3, 4))
+    for k in range(2, seps):
+        stage_b(k)
+    weight_start(1, (1, 2, 3, 4))
+    for n in range(1):
+        weight(0, n).wait_recv()
+        weight(2, n).start()
+
+    chunks = [(k, h) for k in range(seps) for h in range(HALVES)]
+    for step in range(len(chunks) + LAG * (n_z - 1) + 1):
+        if step < len(chunks):
+            stage_c(*chunks[step])
+        for number in range(n_z - 1):
+            j = step - LAG * number
+            if 0 <= j < len(chunks):
+                hop(*chunks[j], number)
+        j = step - LAG * (n_z - 2) - 1
+        if 0 <= j < len(chunks):
+            k, h = chunks[j]
+            finish(k, h)
+            if h == HALVES - 1:
+                if k == 0:
+                    for n in range(1, 5):
+                        weight(0, n).wait_recv()
+                        weight(2, n).start()
+                    for way in (1, 2):
+                        weight(way, 0).wait_recv()
+                if k == 1:
+                    for n in range(1, 5):
+                        for way in (1, 2):
+                            weight(way, n).wait_recv()
+                chain(k)
+
+    last = seps - 1
+    root_rhs_t = g_rr[...].T
+    turned_rr = part.at[0, :, pl.ds(0, zrows)]
+    for k in range(seps):
+        core_copy(k).wait_send()
+    turned_rr[...] = root_rhs_t
+    my_cols = pl.ds(pl.multiple_of(half * c + quarter * y, 8), quarter)
+    wait_along_z(solved.at[last], last)
+    term = dot3(split(solved[last]), split(g_rc[...]), NT)
+    root_send[...] = term
+    swap = remote(root_send, root_recv, x_send.at[0], x_recv.at[0], x_peer)
+    swap.start()
+    for k in range(seps):
+        sep_out[k] = assemble(k)
+    swap.wait_recv()
+    root_full[:, zlanes] = part[0, my_cols, pl.ds(0, zrows)] - (term + root_recv[...])
+    for d in range(1, n_z):
+        along_z(root_full, seps, d, False).start()
+    wait_along_z(root_full, seps)
+    turn(seps, dot3(split(root_full[...]), split(g_ri[...]), NT))
+    root_out[...] = assemble(seps)
+
+    for way in range(3):
+        for n in range(5):
+            weight(way, n).wait_send()
+    for k, h in chunks:
+        y_copy(k, h).wait_send()
+
+        @pl.when(z < n_z - 1)
+        def _():
+            fwd_copy(k, h).wait_send()
+
+        @pl.when(z > 0)
+        def _():
+            bwd_copy(k, h).wait_send()
+
+    for k in range(seps + 1):
+        ref = solved.at[k] if k < seps else root_full
+        for d in range(1, n_z):
+            along_z(ref, k, d, False).wait_send()
+        for n in range(3):
+            out_copy(k, n).wait_send()
+    swap.wait_send()
+
+
+def fused(
+    n_z,
+    leaf_rhs,
+    leaf_inverse,
+    leaf_coupling,
+    parent,
+    sep_rhs,
+    sep_inverse,
+    sep_coupling,
+    root_coupling,
+    root_rhs,
+    root_inverse,
+):
+    seps, rows, right = sep_rhs.shape[1:]
+    width = sep_inverse.shape[3]
+    zrows, half, quarter = width // n_z, right // 2, right // 4
+    f32 = jnp.float32
+    dma = pltpu.SemaphoreType.DMA
+    vmem = pl.BlockSpec(memory_space=pltpu.VMEM)
+    scratch = [
+        (seps, zrows, width),
+        (seps - 1, zrows, width),
+        (zrows, width),
+        (zrows, right),
+        (zrows, width),
+        (seps, right, width),
+        (seps, half, width),
+    ]
+    scratch += [(seps, quarter, width)] * 9
+    scratch += [
+        (zrows, right),
+        (seps + 1, zrows, 128),
+        (seps + 1, 3, rows, 128),
+        (quarter, zrows),
+        (quarter, zrows),
+        (quarter, width),
+    ]
+    sems = [(3, 5)] * 2 + [(seps,)] * 2 + [(seps, HALVES)] * 6
+    sems += [(seps + 1, n_z - 1)] * 2 + [(seps + 1, 3)] * 2 + [(1,)] * 2
+    sep, root = pl.pallas_call(
+        functools.partial(kernel, n_z),
+        out_shape=(
+            jax.ShapeDtypeStruct((seps, rows, right), f32),
+            jax.ShapeDtypeStruct((rows, right), f32),
+        ),
+        in_specs=[pl.BlockSpec(memory_space=pltpu.SMEM)] + [vmem] * 9,
+        out_specs=(vmem, vmem),
+        scratch_shapes=[pltpu.VMEM(s, f32) for s in scratch] + [dma(s) for s in sems],
+        compiler_params=pltpu.CompilerParams(
+            collective_id=0, has_side_effects=True, vmem_limit_bytes=60 * 2**20
+        ),
+        name="forward_solve",
+    )(
+        parent,
+        leaf_rhs.reshape(leaf_rhs.shape[2:]),
+        leaf_inverse.reshape(leaf_inverse.shape[2:]),
+        leaf_coupling.reshape(leaf_coupling.shape[2:]),
+        sep_rhs.reshape(sep_rhs.shape[1:]),
+        sep_inverse.reshape(sep_inverse.shape[1:]),
+        sep_coupling.reshape(sep_coupling.shape[1:]),
+        root_coupling.reshape(root_coupling.shape[1:]),
+        root_rhs,
+        root_inverse,
+    )
+    return sep[None], root
 
 
 def body(
@@ -54,8 +495,23 @@
 
 
 def solution(mesh):
+    n_layer, n_row = mesh.shape["layer"], mesh.shape["row"]
+
+    def per_device(*arrays):
+        right, width = arrays[0].shape[3], arrays[5].shape[3]
+        n_z = n_row // 4
+        fits = (
+            n_layer == 2
+            and n_row in (8, 16)
+            and width % (128 * n_z) == 0
+            and right % (32 * HALVES) == 0
+            and right // 4 <= 128
+            and arrays[4].shape[1] >= 3
+        )
+        return functools.partial(fused, n_z)(*arrays) if fits else body(*arrays)
+
     return jax.shard_map(
-        body,
+        per_device,
         mesh=mesh,
         in_specs=(
             P("layer", "row", None, None),

time: 257 us -> 84.6 us (0.33)
  blocking collectives: 112 us -> 0 us
  waiting for transfers between devices: 107 us -> 0 us
  Pallas kernels: 0 us -> 80 us
  matrix products: 18.8 us -> 0 us
  between operations: 15 us -> 1.29 us
    psum x1 -> x0, waiting for transfers between devices: 107 us -> none  [body(): lax.psum(residual_term(k), 'row')]
    all_gather x5 -> x0, blocking collectives: 104 us -> none  [the longest x4 82.6 us: body(): gathered = lax.all_gather(current, 'row', axis=0, tiled=True)]
    pallas_call x0 -> x1, Pallas kernels: none -> 80 us  [fused(): pl.pallas_call(functools.partial(kernel, n_z), out_shape=(jax.ShapeDtypeS...]
    dot_general x14 -> x0, matrix products: 18.8 us -> none  [the longest x4 10.3 us: residual_term(): jnp.dot(leaf_coupling[0, 0, k], leaf_solution, precision=highest)]
    psum x1 -> x0, blocking collectives: 8.58 us -> none  [body(): root_sum = lax.psum(root_term, 'layer')]
    unnamed x22 -> x2, local copies, waits for them, and re-layouts: 0.06 us -> 3.04 us
  transfers between devices with their start and end apart: 1 -> 0, of which waited for: 1 -> 0; matrix products, arithmetic and copies ran while one was open for 0% -> 0% of each run, Pallas kernels for 0% -> 0%
where the time goes in v1:
time: 84.6 us; the launch traced here: 84.4 us
  Pallas kernels  80 us (95%)
  local copies, waits for them, and re-layouts  3.04 us (4%)
  between operations  1.29 us (2%)
    pallas_call x1, Pallas kernels, fused(): pl.pallas_call(functools.partial(kernel, n_z), out_shape=(jax.ShapeDtypeS...  80 us
    unnamed x2, local copies, waits for them, and re-layouts  3.04 us

profile of v1, /device:TPU:0, one launch (start us, length us, event | category | flops | bytes accessed | tf_op | source)
XLA Modules:
  0.0 84.4 jit_solution(3452989381911556242)
XLA Ops:
  1.3 80.0 %forward_solve.1 = (f32[4,32,384]{2,1,0:T(8,128)}, f32[32,384]{1,0:T(8,128)}) custom-call(s32[1,1]{1,0:T(1,128)S(6)} %copy.14.parent, f32[256,384]{1,0:T(8,128)} %bitcast.9, f32[256,256]{1,0:T(8,128)} %bitcast.10, f32[4,512,256]{2,1,0:T(8,128)} %bitcast.8, f32[4,32,384]{2,1,0:T(8,128)} %bitcast.13, f32[4,32,512]{2,1,0:T(8,128)} %bitcast.11, ...), custom_call_target="tpu_custom_call" | custom-call | tf_op jit(solution)/shard_map/forward_solve/pallas_call | solution.py:420
  81.3 1.6 %copy.15 = f32[1,4,32,384]{3,2,1,0:T(8,128)} copy(f32[1,4,32,384]{3,2,1,0:T(8,128)} %bitcast.12) | data formatting | bytes 393216
  82.9 1.4 %copy.16 = f32[32,384]{1,0:T(8,128)} copy(f32[32,384]{1,0:T(8,128)} %get-tuple-element.9) | data formatting | bytes 98304

commit v2 on v1

--- a/solution.py
+++ b/solution.py
@@ -11,7 +11,7 @@
 NN = (((1,), (0,)), ((), ()))
 NT = (((1,), (1,)), ((), ()))
 HALVES = 2
-LAG = 1
+LAG = 2
 
 
 def split(a):
@@ -297,43 +297,50 @@
     weight_start(1, (0,))
     stage_a(1)
     stage_b(0)
-    stage_a(2)
-    stage_b(1)
-    stage_a(3) if seps > 3 else None
-    weight_start(0, (1, 2, 3, 4))
-    for k in range(2, seps):
-        stage_b(k)
-    weight_start(1, (1, 2, 3, 4))
-    for n in range(1):
-        weight(0, n).wait_recv()
-        weight(2, n).start()
-
     chunks = [(k, h) for k in range(seps) for h in range(HALVES)]
+
+    def ahead(step):
+        k = step // HALVES + 2
+        if step % HALVES == 0 and k < seps:
+            stage_a(k)
+            stage_b(k - 1)
+        if step == HALVES * (seps - 2):
+            stage_b(seps - 1)
+            weight_start(1, (1, 2, 3, 4))
+            weight_start(0, (1, 2, 3, 4))
+            for n in (0,):
+                weight(0, n).wait_recv()
+                weight(2, n).start()
+
     for step in range(len(chunks) + LAG * (n_z - 1) + 1):
-        if step < len(chunks):
-            stage_c(*chunks[step])
-        for number in range(n_z - 1):
+        ahead(step)
+        for number in reversed(range(n_z - 1)):
             j = step - LAG * number
             if 0 <= j < len(chunks):
+                if number == 0:
+                    stage_c(*chunks[j])
                 hop(*chunks[j], number)
-        j = step - LAG * (n_z - 2) - 1
+        j = step - LAG * (n_z - 1)
         if 0 <= j < len(chunks):
             k, h = chunks[j]
             finish(k, h)
             if h == HALVES - 1:
                 if k == 0:
-                    for n in range(1, 5):
+                    weight(0, 1).wait_recv()
+                    weight(2, 1).start()
+                if k < 2:
+                    for way in (1, 2):
+                        weight(way, k).wait_recv()
+                if k == seps - 1:
+                    for n in range(2, 5):
                         weight(0, n).wait_recv()
                         weight(2, n).start()
-                    for way in (1, 2):
-                        weight(way, 0).wait_recv()
-                if k == 1:
-                    for n in range(1, 5):
-                        for way in (1, 2):
-                            weight(way, n).wait_recv()
                 chain(k)
 
     last = seps - 1
+    for n in range(2, 5):
+        for way in (1, 2):
+            weight(way, n).wait_recv()
     root_rhs_t = g_rr[...].T
     turned_rr = part.at[0, :, pl.ds(0, zrows)]
     for k in range(seps):

time: 84.6 us -> 80.4 us (0.950)
  Pallas kernels: 80 us -> 75.9 us
    pallas_call x1, Pallas kernels: 80 us -> 75.9 us  [fused(): pl.pallas_call(functools.partial(kernel, n_z), out_shape=(jax.ShapeDtypeS...]
where the time goes in v2:
time: 80.4 us; the launch traced here: 80.2 us
  Pallas kernels  75.9 us (94%)
  local copies, waits for them, and re-layouts  3.04 us (4%)
  between operations  1.29 us (2%)
    pallas_call x1, Pallas kernels, fused(): pl.pallas_call(functools.partial(kernel, n_z), out_shape=(jax.ShapeDtypeS...  75.9 us
    unnamed x2, local copies, waits for them, and re-layouts  3.04 us

profile of v2, /device:TPU:0, one launch (start us, length us, event | category | flops | bytes accessed | tf_op | source)
XLA Modules:
  0.0 80.2 jit_solution(178943416519764104)
XLA Ops:
  1.3 75.9 %forward_solve.1 = (f32[4,32,384]{2,1,0:T(8,128)}, f32[32,384]{1,0:T(8,128)}) custom-call(s32[1,1]{1,0:T(1,128)S(6)} %copy.14.parent, f32[256,384]{1,0:T(8,128)} %bitcast.9, f32[256,256]{1,0:T(8,128)} %bitcast.10, f32[4,512,256]{2,1,0:T(8,128)} %bitcast.8, f32[4,32,384]{2,1,0:T(8,128)} %bitcast.13, f32[4,32,512]{2,1,0:T(8,128)} %bitcast.11, ...), custom_call_target="tpu_custom_call" | custom-call | tf_op jit(solution)/shard_map/forward_solve/pallas_call | solution.py:427
  77.2 1.6 %copy.15 = f32[1,4,32,384]{3,2,1,0:T(8,128)} copy(f32[1,4,32,384]{3,2,1,0:T(8,128)} %bitcast.12) | data formatting | bytes 393216
  78.8 1.4 %copy.16 = f32[32,384]{1,0:T(8,128)} copy(f32[32,384]{1,0:T(8,128)} %get-tuple-element.9) | data formatting | bytes 98304
